TPU v7x, 32 devices: a whole 2x2x4 slice. The times are simulated.
32 devices in a mesh: row: 8 (over y, x, core), col: 4 (over z).
Axes of the slice: x: 2, y: 2, z: 4, core: 2. Of those that a mesh axis runs over, the one named last changes fastest.
Arguments:
- panel: int32 [32], replicated, may hold values from 0 to 31, each once
- trailing: float32 [8192, 8192], P('row', 'col'), as said below
Outputs:
- factor_panels: float32 [8192, 768], P('row')
- schur: float32 [8192, 8192], P('row', 'col')
Inputs may be any that keep to these rules, and one draw needn't show every extreme that they name: panel names every block index once. In matrix order trailing is symmetric, and each diagonal block of 256 x 256 is strictly diagonally dominant with a positive diagonal.
All inputs are finite; a program needn't handle non-finite values.
Results may differ from a plain program's by a relative error of at most 0.0001.
Values sent between devices are 32-bit elements; how exact they have to be, the bound alone decides.
No kernel may reach another device: no remote copies, remote signals or barrier semaphores. Data moves between devices by JAX's collectives and lax.ppermute only.
A program may use at most 128 MiB of HBM per device.

v0:
```python
import jax
import jax.numpy as jnp
from jax import lax
from jax.sharding import PartitionSpec as P

NB = 256
PANELS = 3


def spread(value, axis, source):
    kept = jnp.where(lax.axis_index(axis) == source, value, 0).astype(value.dtype)
    return lax.psum(kept, axis)


def solve_panel(columns, corner):
    lower = jnp.linalg.cholesky(corner)
    identity = jnp.eye(corner.shape[0], dtype=jnp.float32)
    inverse = lax.linalg.triangular_solve(lower, identity, left_side=True, lower=True)
    return jnp.dot(
        columns, inverse.T, precision=lax.Precision.HIGHEST, preferred_element_type=jnp.float32
    )


def on_device(panel, trailing):
    rows_all = lax.axis_size("row")
    cols_all = lax.axis_size("col")
    my_row = lax.axis_index("row")
    my_col = lax.axis_index("col")
    loc_rows, loc_cols = trailing.shape
    blk_rows = loc_rows // NB
    blk_cols = loc_cols // NB
    ratio = rows_all // cols_all
    row_ids = jnp.arange(loc_rows, dtype=jnp.int32) // NB
    col_ids = jnp.arange(loc_cols, dtype=jnp.int32) // NB
    current = trailing
    factors = []
    for step in range(PANELS):
        pivot = panel[step]
        owner_row = pivot % rows_all
        local_row = pivot // rows_all
        owner_col = pivot % cols_all
        local_col = pivot // cols_all
        columns = lax.dynamic_slice_in_dim(current, local_col * NB, NB, 1)
        corner = lax.dynamic_slice_in_dim(columns, local_row * NB, NB, 0)
        pivot_tile = spread(corner, "row", owner_row)
        row_factor = spread(solve_panel(columns, pivot_tile), "col", owner_col)
        pieces = []
        for offset in range(ratio):
            fetched = spread(row_factor, "row", my_col + offset * cols_all)
            pieces.append(fetched.reshape(blk_rows, NB, NB))
        col_factor = jnp.stack(pieces, axis=1).reshape(blk_cols * NB, NB)
        update = lax.dot_general(
            row_factor,
            col_factor,
            (((1,), (1,)), ((), ())),
            precision=lax.Precision.HIGHEST,
            preferred_element_type=jnp.float32,
        )
        current = current - update
        keep_rows = (row_ids != local_row) | (my_row != owner_row)
        keep_cols = (col_ids != local_col) | (my_col != owner_col)
        current = jnp.where(keep_rows[:, None] & keep_cols[None, :], current, jnp.float32(0.0))
        factors.append(row_factor)
    return (jnp.concatenate(factors, axis=1), current)


def solution(mesh):
    in_specs = (P(), P("row", "col"))
    out_specs = (P("row", None), P("row", "col"))
    return jax.shard_map(
        on_device, mesh=mesh, in_specs=in_specs, out_specs=out_specs, check_vma=False
    )
```

profile of v0, /device:TPU:0, one launch (start us, length us, event | category | flops | bytes accessed | tf_op | source)
XLA Modules:
  0.0 797.8 jit_solution(4477696324197038148)
XLA Ops:
  7.2 1.4 fusion.64
  11.3 9.3 %copy.13 = f32[1024,2048]{0,1:T(8,128)} copy(f32[1024,2048]{1,0:T(8,128)} %param.6) | data formatting | bytes 16777216 | tf_op args[1]
  20.5 1.8 dynamic-slice_select_fusion.2
  22.5 56.7 %all-reduce.14.cloned.1.call-done = f32[256,256]{0,1:T(8,128)} async-done(((f32[256,256]{0,1:T(8,128)}), f32[256,256]{0,1:T(8,128)}) %all-reduce.14.cloned.1.call-update) | async-done | bytes 262160 | tf_op jit(solution)/shard_map/psum | solution.py:12
  79.1 1.1 copy.14
  80.2 1.0 fusion.14
  81.2 11.7 %cholesky.172 = f32[128,128]{1,0:T(8,128)S(1)} custom-call(f32[128,128]{1,0:T(8,128)S(1)} %cholesky.270), custom_call_target="Cholesky" | custom-call | tf_op jit(solution)/shard_map/jit(cholesky)/cholesky | solution.py:16
  93.0 9.8 %custom-call.15 = f32[1,128,128]{1,2,0:T(8,128)S(1)} custom-call(f32[1,128,128]{2,1,0:T(8,128)S(1)} %get-tuple-element.84), custom_call_target="InvertDiagBlocksLowerTriangular" | custom-call | tf_op jit(solution)/shard_map/jit(cholesky)/cholesky | solution.py:16
  103.3 11.7 %cholesky.189 = f32[128,128]{1,0:T(8,128)S(1)} custom-call(f32[128,128]{1,0:T(8,128)S(1)} %convolution_subtract_fusion.5), custom_call_target="Cholesky" | custom-call | tf_op jit(solution)/shard_map/jit(cholesky)/cholesky | solution.py:16
  115.0 0.7 compare_reduce_fusion.4
  117.2 4.3 while.6
  118.0 1.4 bitcast_dynamic-update-slice_fusion.6
  119.5 0.6 fusion.86
  120.1 1.4 bitcast_dynamic-update-slice_fusion.6
  121.5 19.7 %custom-call.16 = f32[2,128,128]{1,2,0:T(8,128)S(1)} custom-call(f32[2,128,128]{2,1,0:T(8,128)S(1)} %get-tuple-element.24), custom_call_target="InvertDiagBlocksLowerTriangular" | custom-call | tf_op jit(solution)/shard_map/triangular_solve/custom-call.0 | solution.py:18
  142.1 3.2 convolution_select_fusion.2
  145.4 51.4 %all-reduce.16.cloned.1.call-done = f32[1024,256]{1,0:T(8,128)} async-done(((f32[1024,256]{1,0:T(8,128)}), f32[1024,256]{1,0:T(8,128)}) %all-reduce.16.cloned.1.call-update) | async-done | bytes 1048592 | tf_op jit(solution)/shard_map/psum | solution.py:12
  196.8 2.7 broadcast_select_fusion.5
  202.5 59.3 %all-reduce.30.cloned.1.call-done = (f32[4,1,256,256]{3,2,1,0:T(8,128)}, f32[4,1,256,256]{3,2,1,0:T(8,128)}) async-done(((f32[4,1,256,256]{3,2,1,0:T(8,128)}, f32[4,1,256,256]{3,2,1,0:T(8,128)}), (f32[4,1,256,256]{3,2,1,0:T(8,128)}, f32[4,1,256,256]{3,2,1,0:T(8,128)})) %all-reduce.30.cloned.1.call-update) | async-done | bytes 2097168 | tf_op jit(solution)/shard_map/psum | solution.py:12
  261.8 1.8 pad_maximum_fusion.1
  263.6 10.4 %subtract_select_fusion.2 = f32[1024,2048]{0,1:T(8,128)S(1)} fusion(f32[1024,2048]{0,1:T(8,128)} %copy.13, f32[1024,256]{1,0:T(8,128)S(1)} %copy-done.2, f32[2048,256]{1,0:T(8,128)S(1)} %bitcast.124, pred[1024]{0:T(1024)(128)(4,1)S(1)} %fusion.51, pred[2048]{0:T(1024)(128)(4,1)S(1)} %fusion.42), kind=kOutput, calls=%fused_computation.8 | convolution fusion | flops 6448742400 | bytes 19926016 | tf_op jit(solution)/shard_map/dot_general | solution.py:52
  274.0 3.4 copy-done
  277.4 0.8 dynamic-slice_select_fusion.1
  278.7 52.6 %all-reduce.18.cloned.1.call-done = f32[256,256]{0,1:T(8,128)} async-done(((f32[256,256]{0,1:T(8,128)}), f32[256,256]{0,1:T(8,128)}) %all-reduce.18.cloned.1.call-update) | async-done | bytes 262160 | tf_op jit(solution)/shard_map/psum | solution.py:12
  331.3 1.1 copy.19
  332.4 1.0 fusion.13
  333.4 11.7 %cholesky.206 = f32[128,128]{1,0:T(8,128)S(1)} custom-call(f32[128,128]{1,0:T(8,128)S(1)} %cholesky.273), custom_call_target="Cholesky" | custom-call | tf_op jit(solution)/shard_map/jit(cholesky)/cholesky | solution.py:16
  345.2 0.6 compare_reduce_fusion.3
  345.8 9.8 %custom-call.17 = f32[1,128,128]{1,2,0:T(8,128)S(1)} custom-call(f32[1,128,128]{2,1,0:T(8,128)S(1)} %get-tuple-element.80), custom_call_target="InvertDiagBlocksLowerTriangular" | custom-call | tf_op jit(solution)/shard_map/jit(cholesky)/cholesky | solution.py:16
  356.1 11.7 %cholesky.223 = f32[128,128]{1,0:T(8,128)S(1)} custom-call(f32[128,128]{1,0:T(8,128)S(1)} %convolution_subtract_fusion.4), custom_call_target="Cholesky" | custom-call | tf_op jit(solution)/shard_map/jit(cholesky)/cholesky | solution.py:16
  367.9 0.7 compare_reduce_fusion.2
  370.0 4.3 while.7
  370.2 0.6 fusion.87
  370.8 1.4 bitcast_dynamic-update-slice_fusion.7
  372.9 1.4 bitcast_dynamic-update-slice_fusion.7
  374.3 19.7 %custom-call.18 = f32[2,128,128]{1,2,0:T(8,128)S(1)} custom-call(f32[2,128,128]{2,1,0:T(8,128)S(1)} %get-tuple-element.25), custom_call_target="InvertDiagBlocksLowerTriangular" | custom-call | tf_op jit(solution)/shard_map/triangular_solve/custom-call.0 | solution.py:18
  394.9 4.0 convolution_select_fusion.1
  399.0 51.4 %all-reduce.20.cloned.1.call-done = f32[1024,256]{1,0:T(8,128)} async-done(((f32[1024,256]{1,0:T(8,128)}), f32[1024,256]{1,0:T(8,128)}) %all-reduce.20.cloned.1.call-update) | async-done | bytes 1048592 | tf_op jit(solution)/shard_map/psum | solution.py:12
  450.4 2.7 broadcast_select_fusion.3
  455.7 59.5 %all-reduce.28.cloned.1.call-done = (f32[4,1,256,256]{3,2,1,0:T(8,128)}, f32[4,1,256,256]{3,2,1,0:T(8,128)}) async-done(((f32[4,1,256,256]{3,2,1,0:T(8,128)}, f32[4,1,256,256]{3,2,1,0:T(8,128)}), (f32[4,1,256,256]{3,2,1,0:T(8,128)}, f32[4,1,256,256]{3,2,1,0:T(8,128)})) %all-reduce.28.cloned.1.call-update) | async-done | bytes 2097168 | tf_op jit(solution)/shard_map/psum | solution.py:12
  515.2 1.8 pad_maximum_fusion.2
  517.0 10.4 %subtract_select_fusion.1 = f32[1024,2048]{0,1:T(8,128)S(1)} fusion(f32[1024,2048]{0,1:T(8,128)} %copy-done, f32[1024,256]{1,0:T(8,128)S(1)} %copy-done.3, f32[2048,256]{1,0:T(8,128)S(1)} %bitcast.125, pred[1024]{0:T(1024)(128)(4,1)S(1)} %fusion.52, pred[2048]{0:T(1024)(128)(4,1)S(1)} %fusion.43), kind=kOutput, calls=%fused_computation.7 | convolution fusion | flops 6448742400 | bytes 19926016 | tf_op jit(solution)/shard_map/dot_general | solution.py:52
  527.4 3.4 copy-done.1
  530.8 0.8 dynamic-slice_select_fusion
  531.9 52.8 %all-reduce.22.cloned.1.call-done = f32[256,256]{0,1:T(8,128)} async-done(((f32[256,256]{0,1:T(8,128)}), f32[256,256]{0,1:T(8,128)}) %all-reduce.22.cloned.1.call-update) | async-done | bytes 262160 | tf_op jit(solution)/shard_map/psum | solution.py:12
  584.7 1.1 copy.23
  585.8 1.0 fusion.12
  586.8 11.7 %cholesky.240 = f32[128,128]{1,0:T(8,128)S(1)} custom-call(f32[128,128]{1,0:T(8,128)S(1)} %cholesky.276), custom_call_target="Cholesky" | custom-call | tf_op jit(solution)/shard_map/jit(cholesky)/cholesky | solution.py:16
  598.5 0.6 compare_reduce_fusion.1
  599.2 9.8 %custom-call.19 = f32[1,128,128]{1,2,0:T(8,128)S(1)} custom-call(f32[1,128,128]{2,1,0:T(8,128)S(1)} %get-tuple-element.76), custom_call_target="InvertDiagBlocksLowerTriangular" | custom-call | tf_op jit(solution)/shard_map/jit(cholesky)/cholesky | solution.py:16
  609.5 11.7 %cholesky.257 = f32[128,128]{1,0:T(8,128)S(1)} custom-call(f32[128,128]{1,0:T(8,128)S(1)} %convolution_subtract_fusion.3), custom_call_target="Cholesky" | custom-call | tf_op jit(solution)/shard_map/jit(cholesky)/cholesky | solution.py:16
  621.3 0.7 compare_reduce_fusion
  623.4 4.4 while.8
  624.3 1.4 bitcast_dynamic-update-slice_fusion.8
  626.3 1.4 bitcast_dynamic-update-slice_fusion.8
  627.7 19.7 %custom-call.20 = f32[2,128,128]{1,2,0:T(8,128)S(1)} custom-call(f32[2,128,128]{2,1,0:T(8,128)S(1)} %get-tuple-element.26), custom_call_target="InvertDiagBlocksLowerTriangular" | custom-call | tf_op jit(solution)/shard_map/triangular_solve/custom-call.0 | solution.py:18
  648.3 4.0 convolution_select_fusion
  652.4 51.4 %all-reduce.24.cloned.1.call-done = f32[1024,256]{1,0:T(8,128)} async-done(((f32[1024,256]{1,0:T(8,128)}), f32[1024,256]{1,0:T(8,128)}) %all-reduce.24.cloned.1.call-update) | async-done | bytes 1048592 | tf_op jit(solution)/shard_map/psum | solution.py:12
  703.8 2.8 broadcast_select_fusion.1
  706.7 1.9 pad_maximum_fusion
  708.6 59.7 %all-reduce.26.cloned.1.call-done = (f32[4,1,256,256]{3,2,1,0:T(8,128)}, f32[4,1,256,256]{3,2,1,0:T(8,128)}) async-done(((f32[4,1,256,256]{3,2,1,0:T(8,128)}, f32[4,1,256,256]{3,2,1,0:T(8,128)}), (f32[4,1,256,256]{3,2,1,0:T(8,128)}, f32[4,1,256,256]{3,2,1,0:T(8,128)})) %all-reduce.26.cloned.1.call-update) | async-done | bytes 2097168 | tf_op jit(solution)/shard_map/psum | solution.py:12
  768.3 1.8 pad_maximum_fusion.3
  770.1 11.7 %subtract_select_fusion = f32[1024,2048]{0,1:T(8,128)} fusion(f32[1024,2048]{0,1:T(8,128)} %copy-done.1, f32[1024,256]{1,0:T(8,128)S(1)} %copy-done.4, f32[2048,256]{1,0:T(8,128)S(1)} %bitcast.123, pred[1024]{0:T(1024)(128)(4,1)S(1)} %fusion.53, pred[2048]{0:T(1024)(128)(4,1)S(1)} %fusion.44), kind=kOutput, calls=%fused_computation.6 | convolution fusion | flops 6448742400 | bytes 19926016 | tf_op jit(solution)/shard_map/dot_general | solution.py:52
  781.8 9.1 %copy.27 = f32[1024,2048]{1,0:T(8,128)} copy(f32[1024,2048]{0,1:T(8,128)} %subtract_select_fusion) | data formatting | bytes 16777216
  (78 shorter events, 8.2 us)
Async XLA Ops:
  7.2 72.0 %all-reduce.14.cloned.1.call-start = ((), (), s32[]{:S(2)}) async-start(), calls=%async_computation | async-start | bytes 524288 | tf_op jit(solution)/shard_map/psum | solution.py:12
  22.4 174.5 %all-reduce.16.cloned.1.call-start = ((), (), s32[]{:S(2)}) async-start(), calls=%async_computation.1 | async-start | bytes 2097152 | tf_op jit(solution)/shard_map/psum | solution.py:12
  145.4 116.5 %all-reduce.30.cloned.1.call-start = ((), (), s32[]{:S(2)}) async-start(), calls=%async_computation.8 | async-start | bytes 4194304 | tf_op jit(solution)/shard_map/psum | solution.py:12
  199.5 64.1 %copy-start.2 = (f32[1024,256]{1,0:T(8,128)S(1)}, f32[1024,256]{1,0:T(8,128)}, u32[]{:S(2)}) copy-start(f32[1024,256]{1,0:T(8,128)} %all-reduce.16.cloned.1.call-done) | copy-start | bytes 3145732
  199.5 131.8 %all-reduce.18.cloned.1.call-start = ((), (), s32[]{:S(2)}) async-start(), calls=%async_computation.2 | async-start | bytes 524288 | tf_op jit(solution)/shard_map/psum | solution.py:12
  274.0 3.4 copy-start
  278.3 172.1 %all-reduce.20.cloned.1.call-start = ((), (), s32[]{:S(2)}) async-start(), calls=%async_computation.3 | async-start | bytes 2097152 | tf_op jit(solution)/shard_map/psum | solution.py:12
  398.9 116.3 %all-reduce.28.cloned.1.call-start = ((), (), s32[]{:S(2)}) async-start(), calls=%async_computation.7 | async-start | bytes 4194304 | tf_op jit(solution)/shard_map/psum | solution.py:12
  453.1 63.9 %copy-start.3 = (f32[1024,256]{1,0:T(8,128)S(1)}, f32[1024,256]{1,0:T(8,128)}, u32[]{:S(2)}) copy-start(f32[1024,256]{1,0:T(8,128)} %all-reduce.20.cloned.1.call-done) | copy-start | bytes 3145732
  453.1 131.6 %all-reduce.22.cloned.1.call-start = ((), (), s32[]{:S(2)}) async-start(), calls=%async_computation.4 | async-start | bytes 524288 | tf_op jit(solution)/shard_map/psum | solution.py:12
  527.4 3.4 copy-start.1
  531.6 172.2 %all-reduce.24.cloned.1.call-start = ((), (), s32[]{:S(2)}) async-start(), calls=%async_computation.5 | async-start | bytes 2097152 | tf_op jit(solution)/shard_map/psum | solution.py:12
  652.4 115.9 %all-reduce.26.cloned.1.call-start = ((), (), s32[]{:S(2)}) async-start(), calls=%async_computation.6 | async-start | bytes 4194304 | tf_op jit(solution)/shard_map/psum | solution.py:12
  703.8 2.9 copy-start.4
Sparse Core Ops, SparseCore 0:
  22.5 56.5 all-reduce.13
  145.5 51.2 all-reduce.15
  200.7 61.1 all-reduce.29
  278.4 52.9 all-reduce.17
  399.0 51.2 all-reduce.19
  454.1 61.1 all-reduce.27
  531.8 52.9 all-reduce.21
  652.5 51.2 all-reduce.23
  707.1 61.1 all-reduce.25
where the time goes:
time: 807 us; the launch traced here: 798 us
  waiting for transfers between devices  495 us (61%)
  other arithmetic  184 us (23%)
  matrix products  47.7 us (6%)
  local copies, waits for them, and re-layouts  42.2 us (5%)
  between operations  26.9 us (3%)
    psum x9, waiting for transfers between devices, spread(): return lax.psum(kept, axis)  495 us
    another operation x20, other arithmetic, solve_panel(): lower = jnp.linalg.cholesky(corner)  103 us
    another operation x7, other arithmetic, solve_panel(): lax.linalg.triangular_solve(lower, identity, left_side=True, lower=True)  59.1 us
    dot_general x3, matrix products, on_device(): lax.dot_general(row_factor, col_factor, (((1,), (1,)), ((), ())), precisi...  32.4 us
    unnamed x12, local copies, waits for them, and re-layouts  25.2 us
  transfers between devices with their start and end apart: 9, of which 9 were waited for; matrix products, arithmetic and copies ran while one was open for 0% of the time, Pallas kernels for 0%

commit v1 on v0

--- a/solution.py
+++ b/solution.py
@@ -9,7 +9,7 @@
 
 def spread(value, axis, source):
     kept = jnp.where(lax.axis_index(axis) == source, value, 0).astype(value.dtype)
-    return lax.psum(kept, axis)
+    return jnp.sum(lax.all_gather(kept, axis), axis=0)
 
 
 def solve_panel(columns, corner):

time: 807 us -> 954 us (1.18)
  waiting for transfers between devices: 495 us -> 636 us
  other arithmetic: 184 us -> 213 us
  local copies, waits for them, and re-layouts: 42.2 us -> 20.9 us
    all_gather x0 -> x12, waiting for transfers between devices: none -> 634 us  [spread(): return jnp.sum(lax.all_gather(kept, axis), axis=0)]
    psum x9 -> x0, waiting for transfers between devices: 495 us -> none  [spread(): return lax.psum(kept, axis)]
    reduce_sum x0 -> x12, other arithmetic: none -> 38.4 us  [spread(): return jnp.sum(lax.all_gather(kept, axis), axis=0)]
    unnamed x12 -> x4, local copies, waits for them, and re-layouts: 25.2 us -> 6.78 us
  transfers between devices with their start and end apart: 9 -> 12, of which waited for: 9 -> 12; matrix products, arithmetic and copies ran while one was open for 0% -> 1% of each run, Pallas kernels for 0% -> 0%
where the time goes in v1:
time: 954 us; the launch traced here: 945 us
  waiting for transfers between devices  636 us (67%)
  other arithmetic  213 us (22%)
  matrix products  46.2 us (5%)
  between operations  27 us (3%)
  local copies, waits for them, and re-layouts  20.9 us (2%)
    all_gather x12, waiting for transfers between devices, spread(): return jnp.sum(lax.all_gather(kept, axis), axis=0)  634 us
    another operation x20, other arithmetic, solve_panel(): lower = jnp.linalg.cholesky(corner)  103 us
    another operation x7, other arithmetic, solve_panel(): lax.linalg.triangular_solve(lower, identity, left_side=True, lower=True)  59.1 us
    reduce_sum x12, other arithmetic, spread(): return jnp.sum(lax.all_gather(kept, axis), axis=0)  38.4 us
    dot_general x3, matrix products, on_device(): lax.dot_general(row_factor, col_factor, (((1,), (1,)), ((), ())), precisi...  32.5 us
  transfers between devices with their start and end apart: 12, of which 12 were waited for; matrix products, arithmetic and copies ran while one was open for 1% of the time, Pallas kernels for 0%

profile of v1, /device:TPU:0, one launch (start us, length us, event | category | flops | bytes accessed | tf_op | source)
XLA Modules:
  0.0 944.9 jit_solution(6562544745476999213)
XLA Ops:
  7.2 1.4 fusion.64
  11.3 1.9 dynamic-slice_select_fusion.2
  13.3 30.6 %all-gather.25.cloned.1.call-done = f32[2048,256]{1,0:T(8,128)} async-done(((f32[256,256]{1,0:T(8,128)}), f32[2048,256]{1,0:T(8,128)}) %all-gather.25.cloned.1.call-update) | async-done | bytes 2097168 | tf_op jit(solution)/shard_map/all_gather | solution.py:12
  43.8 1.8 reduce_sum.108
  45.8 11.7 %cholesky.172 = f32[128,128]{1,0:T(8,128)S(1)} custom-call(f32[128,128]{1,0:T(8,128)S(1)} %cholesky.270), custom_call_target="Cholesky" | custom-call | tf_op jit(solution)/shard_map/jit(cholesky)/cholesky | solution.py:16
  57.5 9.8 %custom-call.15 = f32[1,128,128]{1,2,0:T(8,128)S(1)} custom-call(f32[1,128,128]{2,1,0:T(8,128)S(1)} %get-tuple-element.74), custom_call_target="InvertDiagBlocksLowerTriangular" | custom-call | tf_op jit(solution)/shard_map/jit(cholesky)/cholesky | solution.py:16
  67.8 11.7 %cholesky.189 = f32[128,128]{1,0:T(8,128)S(1)} custom-call(f32[128,128]{1,0:T(8,128)S(1)} %convolution_subtract_fusion.5), custom_call_target="Cholesky" | custom-call | tf_op jit(solution)/shard_map/jit(cholesky)/cholesky | solution.py:16
  79.6 0.7 compare_reduce_fusion.4
  81.8 4.3 while.6
  82.6 1.4 bitcast_dynamic-update-slice_fusion.6
  84.7 1.4 bitcast_dynamic-update-slice_fusion.6
  86.1 19.7 %custom-call.16 = f32[2,128,128]{1,2,0:T(8,128)S(1)} custom-call(f32[2,128,128]{2,1,0:T(8,128)S(1)} %get-tuple-element.24), custom_call_target="InvertDiagBlocksLowerTriangular" | custom-call | tf_op jit(solution)/shard_map/triangular_solve/custom-call.0 | solution.py:18
  106.7 3.2 convolution_select_fusion.2
  110.0 80.8 %all-gather.27.cloned.1.call-done = f32[4096,256]{1,0:T(8,128)} async-done(((f32[1024,256]{1,0:T(8,128)}), f32[4096,256]{1,0:T(8,128)}) %all-gather.27.cloned.1.call-update) | async-done | bytes 4194320 | tf_op jit(solution)/shard_map/all_gather | solution.py:12
  190.8 2.6 reduce_sum.109
  193.4 1.5 broadcast_select_fusion.5
  197.9 49.9 %all-gather.29.cloned.1.call-done = f32[8192,256]{1,0:T(8,128)} async-done(((f32[1024,256]{1,0:T(8,128)}), f32[8192,256]{1,0:T(8,128)}) %all-gather.29.cloned.1.call-update) | async-done | bytes 8388624 | tf_op jit(solution)/shard_map/all_gather | solution.py:12
  247.8 4.1 reduce_sum.110
  251.9 52.5 %all-gather.31.cloned.1.call-done = f32[8192,256]{1,0:T(8,128)} async-done(((f32[1024,256]{1,0:T(8,128)}), f32[8192,256]{1,0:T(8,128)}) %all-gather.31.cloned.1.call-update) | async-done | bytes 8388624 | tf_op jit(solution)/shard_map/all_gather | solution.py:12
  304.4 4.1 reduce_sum.111
  308.7 10.4 %subtract_select_fusion.2 = f32[1024,2048]{1,0:T(8,128)S(1)} fusion(f32[1024,2048]{1,0:T(8,128)} %param.6, f32[1024,256]{1,0:T(8,128)S(1)} %reduce_sum.109, f32[2048,256]{1,0:T(8,128)S(1)} %bitcast.131, pred[2048]{0:T(1024)(128)(4,1)S(1)} %fusion.42, pred[1024]{0:T(1024)(128)(4,1)S(1)} %fusion.51), kind=kOutput, calls=%fused_computation.8 | convolution fusion | flops 6448742400 | bytes 19926016 | tf_op jit(solution)/shard_map/dot_general | solution.py:52
  319.1 3.4 copy-done
  322.5 0.8 dynamic-slice_select_fusion.1
  323.8 27.5 %all-gather.33.cloned.1.call-done = f32[2048,256]{1,0:T(8,128)} async-done(((f32[256,256]{1,0:T(8,128)}), f32[2048,256]{1,0:T(8,128)}) %all-gather.33.cloned.1.call-update) | async-done | bytes 2097168 | tf_op jit(solution)/shard_map/all_gather | solution.py:12
  351.3 1.8 reduce_sum.112
  353.3 11.7 %cholesky.206 = f32[128,128]{1,0:T(8,128)S(1)} custom-call(f32[128,128]{1,0:T(8,128)S(1)} %cholesky.273), custom_call_target="Cholesky" | custom-call | tf_op jit(solution)/shard_map/jit(cholesky)/cholesky | solution.py:16
  365.0 9.8 %custom-call.17 = f32[1,128,128]{1,2,0:T(8,128)S(1)} custom-call(f32[1,128,128]{2,1,0:T(8,128)S(1)} %get-tuple-element.70), custom_call_target="InvertDiagBlocksLowerTriangular" | custom-call | tf_op jit(solution)/shard_map/jit(cholesky)/cholesky | solution.py:16
  375.3 11.7 %cholesky.223 = f32[128,128]{1,0:T(8,128)S(1)} custom-call(f32[128,128]{1,0:T(8,128)S(1)} %convolution_subtract_fusion.4), custom_call_target="Cholesky" | custom-call | tf_op jit(solution)/shard_map/jit(cholesky)/cholesky | solution.py:16
  389.8 4.3 while.7
  390.6 1.4 bitcast_dynamic-update-slice_fusion.7
  392.7 1.4 bitcast_dynamic-update-slice_fusion.7
  394.1 19.7 %custom-call.18 = f32[2,128,128]{1,2,0:T(8,128)S(1)} custom-call(f32[2,128,128]{2,1,0:T(8,128)S(1)} %get-tuple-element.25), custom_call_target="InvertDiagBlocksLowerTriangular" | custom-call | tf_op jit(solution)/shard_map/triangular_solve/custom-call.0 | solution.py:18
  414.7 3.2 convolution_select_fusion.1
  418.0 80.8 %all-gather.35.cloned.1.call-done = f32[4096,256]{1,0:T(8,128)} async-done(((f32[1024,256]{1,0:T(8,128)}), f32[4096,256]{1,0:T(8,128)}) %all-gather.35.cloned.1.call-update) | async-done | bytes 4194320 | tf_op jit(solution)/shard_map/all_gather | solution.py:12
  498.8 2.6 reduce_sum.113
  501.4 1.5 broadcast_select_fusion.3
  506.6 49.3 %all-gather.37.cloned.1.call-done = f32[8192,256]{1,0:T(8,128)} async-done(((f32[1024,256]{1,0:T(8,128)}), f32[8192,256]{1,0:T(8,128)}) %all-gather.37.cloned.1.call-update) | async-done | bytes 8388624 | tf_op jit(solution)/shard_map/all_gather | solution.py:12
  555.8 4.1 reduce_sum.114
  559.9 52.1 %all-gather.39.cloned.1.call-done = f32[8192,256]{1,0:T(8,128)} async-done(((f32[1024,256]{1,0:T(8,128)}), f32[8192,256]{1,0:T(8,128)}) %all-gather.39.cloned.1.call-update) | async-done | bytes 8388624 | tf_op jit(solution)/shard_map/all_gather | solution.py:12
  612.0 5.0 reduce_sum.115
  617.0 1.4 pad_maximum_fusion.2
  618.5 10.4 %subtract_select_fusion.1 = f32[1024,2048]{1,0:T(8,128)S(1)} fusion(f32[1024,2048]{1,0:T(8,128)} %copy-done, f32[1024,256]{1,0:T(8,128)S(1)} %reduce_sum.113, f32[2048,256]{1,0:T(8,128)S(1)} %bitcast.130, pred[2048]{0:T(1024)(128)(4,1)S(1)} %fusion.43, pred[1024]{0:T(1024)(128)(4,1)S(1)} %fusion.52), kind=kOutput, calls=%fused_computation.7 | convolution fusion | flops 6448742400 | bytes 19926016 | tf_op jit(solution)/shard_map/dot_general | solution.py:52
  628.9 3.4 copy-done.1
  632.3 0.8 dynamic-slice_select_fusion
  633.4 27.6 %all-gather.41.cloned.1.call-done = f32[2048,256]{1,0:T(8,128)} async-done(((f32[256,256]{1,0:T(8,128)}), f32[2048,256]{1,0:T(8,128)}) %all-gather.41.cloned.1.call-update) | async-done | bytes 2097168 | tf_op jit(solution)/shard_map/all_gather | solution.py:12
  661.1 1.8 reduce_sum.116
  663.0 11.7 %cholesky.240 = f32[128,128]{1,0:T(8,128)S(1)} custom-call(f32[128,128]{1,0:T(8,128)S(1)} %cholesky.276), custom_call_target="Cholesky" | custom-call | tf_op jit(solution)/shard_map/jit(cholesky)/cholesky | solution.py:16
  674.8 9.8 %custom-call.19 = f32[1,128,128]{1,2,0:T(8,128)S(1)} custom-call(f32[1,128,128]{2,1,0:T(8,128)S(1)} %get-tuple-element.66), custom_call_target="InvertDiagBlocksLowerTriangular" | custom-call | tf_op jit(solution)/shard_map/jit(cholesky)/cholesky | solution.py:16
  685.1 11.7 %cholesky.257 = f32[128,128]{1,0:T(8,128)S(1)} custom-call(f32[128,128]{1,0:T(8,128)S(1)} %convolution_subtract_fusion.3), custom_call_target="Cholesky" | custom-call | tf_op jit(solution)/shard_map/jit(cholesky)/cholesky | solution.py:16
  696.9 0.7 compare_reduce_fusion
  699.6 4.4 while.8
  700.5 1.4 bitcast_dynamic-update-slice_fusion.8
  702.5 1.4 bitcast_dynamic-update-slice_fusion.8
  704.0 19.7 %custom-call.20 = f32[2,128,128]{1,2,0:T(8,128)S(1)} custom-call(f32[2,128,128]{2,1,0:T(8,128)S(1)} %get-tuple-element.26), custom_call_target="InvertDiagBlocksLowerTriangular" | custom-call | tf_op jit(solution)/shard_map/triangular_solve/custom-call.0 | solution.py:18
  724.6 3.2 convolution_select_fusion
  727.9 80.8 %all-gather.43.cloned.1.call-done = f32[4096,256]{1,0:T(8,128)} async-done(((f32[1024,256]{1,0:T(8,128)}), f32[4096,256]{1,0:T(8,128)}) %all-gather.43.cloned.1.call-update) | async-done | bytes 4194320 | tf_op jit(solution)/shard_map/all_gather | solution.py:12
  808.7 2.6 reduce_sum.117
  811.3 1.5 broadcast_select_fusion.1
  813.4 1.9 pad_maximum_fusion
  815.3 50.4 %all-gather.45.cloned.1.call-done = f32[8192,256]{1,0:T(8,128)} async-done(((f32[1024,256]{1,0:T(8,128)}), f32[8192,256]{1,0:T(8,128)}) %all-gather.45.cloned.1.call-update) | async-done | bytes 8388624 | tf_op jit(solution)/shard_map/all_gather | solution.py:12
  865.7 4.1 reduce_sum.118
  869.8 52.0 %all-gather.47.cloned.1.call-done = f32[8192,256]{1,0:T(8,128)} async-done(((f32[1024,256]{1,0:T(8,128)}), f32[8192,256]{1,0:T(8,128)}) %all-gather.47.cloned.1.call-update) | async-done | bytes 8388624 | tf_op jit(solution)/shard_map/all_gather | solution.py:12
  921.8 4.1 reduce_sum.119
  926.0 11.6 %subtract_select_fusion = f32[1024,2048]{1,0:T(8,128)} fusion(f32[1024,2048]{1,0:T(8,128)} %copy-done.1, f32[1024,256]{1,0:T(8,128)S(1)} %reduce_sum.117, f32[2048,256]{1,0:T(8,128)S(1)} %bitcast.129, pred[2048]{0:T(1024)(128)(4,1)S(1)} %fusion.44, pred[1024]{0:T(1024)(128)(4,1)S(1)} %fusion.53), kind=kOutput, calls=%fused_computation.6 | convolution fusion | flops 6448742400 | bytes 19926016 | tf_op jit(solution)/shard_map/dot_general | solution.py:52
  (91 shorter events, 14.1 us)
Async XLA Ops:
  7.2 36.7 %all-gather.25.cloned.1.call-start = ((), (), s32[]{:S(2)}) async-start(), calls=%async_computation | async-start | bytes 2359296 | tf_op jit(solution)/shard_map/all_gather | solution.py:12
  13.2 177.7 %all-gather.27.cloned.1.call-start = ((), (), s32[]{:S(2)}) async-start(), calls=%async_computation.1 | async-start | bytes 5242880 | tf_op jit(solution)/shard_map/all_gather | solution.py:12
  109.9 137.9 %all-gather.29.cloned.1.call-start = ((), (), s32[]{:S(2)}) async-start(), calls=%async_computation.2 | async-start | bytes 9437184 | tf_op jit(solution)/shard_map/all_gather | solution.py:12
  194.9 109.5 %all-gather.31.cloned.1.call-start = ((), (), s32[]{:S(2)}) async-start(), calls=%async_computation.3 | async-start | bytes 9437184 | tf_op jit(solution)/shard_map/all_gather | solution.py:12
  195.5 155.8 %all-gather.33.cloned.1.call-start = ((), (), s32[]{:S(2)}) async-start(), calls=%async_computation.4 | async-start | bytes 2359296 | tf_op jit(solution)/shard_map/all_gather | solution.py:12
  319.1 3.4 copy-start
  323.4 175.5 %all-gather.35.cloned.1.call-start = ((), (), s32[]{:S(2)}) async-start(), calls=%async_computation.5 | async-start | bytes 5242880 | tf_op jit(solution)/shard_map/all_gather | solution.py:12
  417.9 137.9 %all-gather.37.cloned.1.call-start = ((), (), s32[]{:S(2)}) async-start(), calls=%async_computation.6 | async-start | bytes 9437184 | tf_op jit(solution)/shard_map/all_gather | solution.py:12
  502.9 109.1 %all-gather.39.cloned.1.call-start = ((), (), s32[]{:S(2)}) async-start(), calls=%async_computation.7 | async-start | bytes 9437184 | tf_op jit(solution)/shard_map/all_gather | solution.py:12
  503.7 157.4 %all-gather.41.cloned.1.call-start = ((), (), s32[]{:S(2)}) async-start(), calls=%async_computation.8 | async-start | bytes 2359296 | tf_op jit(solution)/shard_map/all_gather | solution.py:12
  628.9 3.4 copy-start.1
  633.1 175.5 %all-gather.43.cloned.1.call-start = ((), (), s32[]{:S(2)}) async-start(), calls=%async_computation.9 | async-start | bytes 5242880 | tf_op jit(solution)/shard_map/all_gather | solution.py:12
  727.8 137.9 %all-gather.45.cloned.1.call-start = ((), (), s32[]{:S(2)}) async-start(), calls=%async_computation.10 | async-start | bytes 9437184 | tf_op jit(solution)/shard_map/all_gather | solution.py:12
  812.8 108.9 %all-gather.47.cloned.1.call-start = ((), (), s32[]{:S(2)}) async-start(), calls=%async_computation.11 | async-start | bytes 9437184 | tf_op jit(solution)/shard_map/all_gather | solution.py:12
Sparse Core Ops, SparseCore 0:
  13.3 30.4 all-gather.24
  110.0 80.7 all-gather.26
  195.0 52.7 all-gather.28
  250.1 54.2 all-gather.30
  323.5 27.7 all-gather.32
  418.1 80.7 all-gather.34
  503.1 52.7 all-gather.36
  557.7 54.2 all-gather.38
  633.3 27.7 all-gather.40
  727.9 80.7 all-gather.42
  812.9 52.7 all-gather.44
  867.5 54.2 all-gather.46
